TPU v7x, 32 devices: a whole 2x2x4 slice. The times are simulated.
32 devices in a mesh: dp: 8 (over y, x, core), tensor: 4 (over z).
Axes of the slice: x: 2, y: 2, z: 4, core: 2. Of those that a mesh axis runs over, the one named last changes fastest.
Arguments:
- inputs: bfloat16 [8192, 1024], P(('dp', 'tensor')), may hold values from -6 to 6
- segments: int32 [8, 1024], P('dp'), may hold values from 0 to 3, never falling along the last dimension, each value on 1 to 512 neighbouring positions
- query_weight: bfloat16 [1024, 1024], P(None, 'tensor'), may hold values from -0.1875 to 0.1875
- key_weight: bfloat16 [1024, 1024], P(None, 'tensor'), may hold values from -0.1875 to 0.1875
- value_weight: bfloat16 [1024, 1024], P(None, 'tensor'), may hold values from -0.1875 to 0.1875
- gate_weight: bfloat16 [1024, 1024], P(None, 'tensor'), may hold values from -0.1875 to 0.1875
- out_weight: bfloat16 [1024, 1024], P('tensor'), may hold values from -0.1875 to 0.1875
- left_weight: bfloat16 [1024, 2816], P(None, 'tensor'), may hold values from -0.1875 to 0.1875
- right_weight: bfloat16 [1024, 2816], P(None, 'tensor'), may hold values from -0.1875 to 0.1875
- down_weight: bfloat16 [2816, 1024], P('tensor'), may hold values from -0.109375 to 0.109375
- norm_first: float32 [1024], replicated, may hold values from 0.1 to 1.9
- norm_second: float32 [1024], replicated, may hold values from 0.1 to 1.9
- cotangent: bfloat16 [8192, 1024], P(('dp', 'tensor')), may hold values from -6 to 6
Outputs:
- block_out: bfloat16 [8192, 1024], P(('dp', 'tensor'))
- block_grad: bfloat16 [8192, 1024], P(('dp', 'tensor'))
- query_grad: float32 [1024, 1024], P(None, 'tensor')
- key_grad: float32 [1024, 1024], P(None, 'tensor')
- value_grad: float32 [1024, 1024], P(None, 'tensor')
- gate_grad: float32 [1024, 1024], P(None, 'tensor')
- out_grad: float32 [1024, 1024], P('tensor')
- left_grad: float32 [1024, 2816], P(None, 'tensor')
- right_grad: float32 [1024, 2816], P(None, 'tensor')
- down_grad: float32 [2816, 1024], P('tensor')
- first_grad: float32 [1024], replicated
- second_grad: float32 [1024], replicated
Inputs may be any that keep to these rules, and one draw needn't show every extreme that they name: `segments`: each row holds 4 documents; numbers never fall along a row; each document has 1 to 512 tokens and one of each row exactly 512.
All inputs are finite; a program needn't handle non-finite values.
Results may differ from a plain program's by a relative error of at most 0.02.
Values may be sent and summed in bfloat16 or wider, within the bound.
A program may use at most 128 MiB of HBM per device.

v0:
```python
import jax
import jax.numpy as jnp
from jax import lax
from jax.sharding import PartitionSpec as P

D = 1024
HEADS = 16
EPS = 1e-05


def rms_scale(values):
    return lax.rsqrt(jnp.mean(values * values, axis=-1, keepdims=True) + EPS)


def norm_back(grad_normed, values, scale, gain):
    weighted = grad_normed * gain
    return scale * weighted - values * scale * scale * scale * jnp.mean(
        weighted * values, axis=-1, keepdims=True
    )


def attention_scores(query_pos, key_pos, doc_mask):
    raw_scores = jnp.einsum(
        "rthd,rshd->rhts", query_pos, key_pos, preferred_element_type=jnp.float32
    )
    return jnp.where(doc_mask[:, None], raw_scores, 0.0).astype(jnp.bfloat16)


def per_device(
    inputs,
    segments,
    query_weight,
    key_weight,
    value_weight,
    gate_weight,
    out_weight,
    left_weight,
    right_weight,
    down_weight,
    norm_first,
    norm_second,
    cotangent,
):
    own_rows = inputs.astype(jnp.float32)
    rows_here, length = segments.shape
    all_tokens = rows_here * length
    local_width = query_weight.shape[1]
    head_size = D // HEADS
    heads_here = local_width // head_size
    four_shape = (rows_here, length, heads_here, head_size)
    scale_one = rms_scale(own_rows)
    normed_own = (own_rows * scale_one * norm_first).astype(jnp.bfloat16)
    normed_all = lax.all_gather(normed_own, "tensor", axis=0, tiled=True)
    joined_weight = jnp.concatenate((query_weight, key_weight, value_weight, gate_weight), axis=1)
    projected = jnp.dot(normed_all, joined_weight, preferred_element_type=jnp.float32)
    query_raw = projected[:, :local_width]
    key_raw = projected[:, local_width : 2 * local_width]
    value_raw = projected[:, 2 * local_width : 3 * local_width]
    gate_raw = projected[:, 3 * local_width :]
    query_pos = jax.nn.softplus(query_raw).astype(jnp.bfloat16).reshape(four_shape)
    key_pos = jax.nn.softplus(key_raw).astype(jnp.bfloat16).reshape(four_shape)
    value_pos = value_raw.astype(jnp.bfloat16).reshape(four_shape)
    later = lax.broadcasted_iota(jnp.int32, (length, length), 0) >= lax.broadcasted_iota(
        jnp.int32, (length, length), 1
    )
    doc_mask = (segments[:, :, None] == segments[:, None, :]) & later[None]
    scores = attention_scores(query_pos, key_pos, doc_mask)
    mixed_heads = jnp.einsum(
        "rhts,rshd->rthd", scores, value_pos, preferred_element_type=jnp.float32
    )
    head_scale = rms_scale(mixed_heads)
    head_norm = (mixed_heads * head_scale).reshape(all_tokens, local_width)
    gate_open = jax.nn.sigmoid(gate_raw)
    gated = (head_norm * gate_open).astype(jnp.bfloat16)
    branch = lax.psum_scatter(
        jnp.dot(gated, out_weight, preferred_element_type=jnp.float32).astype(jnp.bfloat16),
        "tensor",
        scatter_dimension=0,
        tiled=True,
    ).astype(jnp.float32)
    residual = own_rows + branch
    scale_two = rms_scale(residual)
    second_own = (residual * scale_two * norm_second).astype(jnp.bfloat16)
    second_all = lax.all_gather(second_own, "tensor", axis=0, tiled=True)
    left_out = jnp.dot(second_all, left_weight, preferred_element_type=jnp.float32)
    right_out = jnp.dot(second_all, right_weight, preferred_element_type=jnp.float32)
    product = (left_out * right_out).astype(jnp.bfloat16)
    ffn_share = lax.psum_scatter(
        jnp.dot(product, down_weight, preferred_element_type=jnp.float32).astype(jnp.bfloat16),
        "tensor",
        scatter_dimension=0,
        tiled=True,
    ).astype(jnp.float32)
    block_out = (residual + ffn_share).astype(jnp.bfloat16)
    upstream = cotangent.astype(jnp.float32)
    down_in = lax.all_gather(cotangent, "tensor", axis=0, tiled=True)
    down_grad = jnp.einsum("tf,td->fd", product, down_in, preferred_element_type=jnp.float32)
    prod_grad = jnp.einsum("td,fd->tf", down_in, down_weight, preferred_element_type=jnp.float32)
    left_back = (prod_grad * right_out).astype(jnp.bfloat16)
    right_back = (prod_grad * left_out).astype(jnp.bfloat16)
    left_grad = jnp.einsum("tc,tf->cf", second_all, left_back, preferred_element_type=jnp.float32)
    right_grad = jnp.einsum("tc,tf->cf", second_all, right_back, preferred_element_type=jnp.float32)
    second_back = lax.psum_scatter(
        (
            jnp.einsum("tf,cf->tc", left_back, left_weight, preferred_element_type=jnp.float32)
            + jnp.einsum("tf,cf->tc", right_back, right_weight, preferred_element_type=jnp.float32)
        ).astype(jnp.bfloat16),
        "tensor",
        scatter_dimension=0,
        tiled=True,
    ).astype(jnp.float32)
    second_part = jnp.sum(second_back * residual * scale_two, axis=0)
    resid_grad = upstream + norm_back(second_back, residual, scale_two, norm_second)
    mixer_in = lax.all_gather(resid_grad.astype(jnp.bfloat16), "tensor", axis=0, tiled=True)
    out_grad = jnp.einsum("tc,td->cd", gated, mixer_in, preferred_element_type=jnp.float32)
    gated_back = jnp.einsum("td,cd->tc", mixer_in, out_weight, preferred_element_type=jnp.float32)
    gate_back = (gated_back * head_norm * gate_open * (1.0 - gate_open)).astype(jnp.bfloat16)
    norm_grad = (gated_back * gate_open).reshape(four_shape)
    mixed_back = (
        head_scale * norm_grad
        - mixed_heads
        * head_scale
        * head_scale
        * head_scale
        * jnp.mean(norm_grad * mixed_heads, axis=-1, keepdims=True)
    ).astype(jnp.bfloat16)
    scores_again = attention_scores(query_pos, key_pos, doc_mask)
    value_back = jnp.einsum(
        "rhts,rthd->rshd", scores_again, mixed_back, preferred_element_type=jnp.float32
    ).astype(jnp.bfloat16)
    score_back = jnp.einsum(
        "rthd,rshd->rhts", mixed_back, value_pos, preferred_element_type=jnp.float32
    )
    score_back = jnp.where(doc_mask[:, None], score_back, 0.0).astype(jnp.bfloat16)
    query_back = jnp.einsum(
        "rhts,rshd->rthd", score_back, key_pos, preferred_element_type=jnp.float32
    )
    query_back = (query_back * jax.nn.sigmoid(query_raw.reshape(four_shape))).astype(jnp.bfloat16)
    key_back = jnp.einsum(
        "rhts,rthd->rshd", score_back, query_pos, preferred_element_type=jnp.float32
    )
    key_back = (key_back * jax.nn.sigmoid(key_raw.reshape(four_shape))).astype(jnp.bfloat16)
    back_all = jnp.concatenate(
        (
            query_back.reshape(all_tokens, local_width),
            key_back.reshape(all_tokens, local_width),
            value_back.reshape(all_tokens, local_width),
            gate_back,
        ),
        axis=1,
    )
    joined_grad = jnp.einsum("tc,tq->cq", normed_all, back_all, preferred_element_type=jnp.float32)
    query_grad = joined_grad[:, :local_width]
    key_grad = joined_grad[:, local_width : 2 * local_width]
    value_grad = joined_grad[:, 2 * local_width : 3 * local_width]
    gate_grad = joined_grad[:, 3 * local_width :]
    first_back = lax.psum_scatter(
        jnp.einsum("tq,cq->tc", back_all, joined_weight, preferred_element_type=jnp.float32).astype(
            jnp.bfloat16
        ),
        "tensor",
        scatter_dimension=0,
        tiled=True,
    ).astype(jnp.float32)
    first_part = jnp.sum(first_back * own_rows * scale_one, axis=0)
    block_grad = (resid_grad + norm_back(first_back, own_rows, scale_one, norm_first)).astype(
        jnp.bfloat16
    )
    query_grad, key_grad, value_grad, gate_grad, out_grad, left_grad, right_grad, down_grad = (
        total.astype(jnp.float32)
        for total in lax.psum(
            tuple(
                (
                    part.astype(jnp.bfloat16)
                    for part in (
                        query_grad,
                        key_grad,
                        value_grad,
                        gate_grad,
                        out_grad,
                        left_grad,
                        right_grad,
                        down_grad,
                    )
                )
            ),
            "dp",
        )
    )
    first_grad, second_grad = lax.psum((first_part, second_part), ("dp", "tensor"))
    return (
        block_out,
        block_grad,
        query_grad,
        key_grad,
        value_grad,
        gate_grad,
        out_grad,
        left_grad,
        right_grad,
        down_grad,
        first_grad,
        second_grad,
    )


def solution(mesh):
    return jax.shard_map(
        per_device,
        mesh=mesh,
        in_specs=(
            P(("dp", "tensor"), None),
            P("dp", None),
            P(None, "tensor"),
            P(None, "tensor"),
            P(None, "tensor"),
            P(None, "tensor"),
            P("tensor", None),
            P(None, "tensor"),
            P(None, "tensor"),
            P("tensor", None),
            P(),
            P(),
            P(("dp", "tensor"), None),
        ),
        out_specs=(
            P(("dp", "tensor"), None),
            P(("dp", "tensor"), None),
            P(None, "tensor"),
            P(None, "tensor"),
            P(None, "tensor"),
            P(None, "tensor"),
            P("tensor", None),
            P(None, "tensor"),
            P(None, "tensor"),
            P("tensor", None),
            P(),
            P(),
        ),
        check_vma=False,
    )
```

profile of v0, /device:TPU:0, one launch (start us, length us, event | category | flops | bytes accessed | tf_op | source)
XLA Modules:
  0.0 557.3 jit_solution(13068382878314407634)
XLA Ops:
  7.3 1.4 fusion.21
  8.7 0.6 copy-done.43
  9.2 2.0 fusion.10
  11.6 0.7 copy-done.33
  12.4 1.3 copy-done.35
  13.7 0.6 fusion
  14.3 45.8 %all-gather.5.cloned.1.call-done = bf16[1024,1024]{1,0:T(8,128)(2,1)} async-done(((bf16[256,1024]{1,0:T(8,128)(2,1)}), bf16[1024,1024]{1,0:T(8,128)(2,1)}) %all-gather.5.cloned.1.call-update) | async-done | bytes 2097168 | tf_op jit(solution)/shard_map/all_gather | solution.py:53
  60.1 4.7 fusion.40
  64.9 1.1 fusion.26
  66.1 2.6 select_convert_fusion.1
  68.8 2.7 multiply_reduce_fusion.2
  71.5 0.6 copy-done.1
  72.2 1.0 copy-done.11
  73.1 0.3 fusion.30
  73.5 0.8 copy-done.15
  74.3 2.1 convolution_convert_fusion.2
  76.4 42.7 %reduce-scatter.5.cloned.1.call-done = bf16[256,1024]{1,0:T(8,128)(2,1)} async-done(((bf16[1024,1024]{1,0:T(8,128)(2,1)}), bf16[256,1024]{1,0:T(8,128)(2,1)}) %reduce-scatter.5.cloned.1.call-update) | async-done | bytes 524304 | tf_op jit(solution)/shard_map/reduce_scatter | solution.py:75
  119.1 1.3 multiply_reduce_fusion.1
  120.4 2.0 multiply_convert_fusion.3
  122.5 0.5 all-gather.9.cloned.1.call-update
  123.0 0.5 reduce-scatter.9.cloned.1.call-start
  123.6 44.3 %all-gather.7.cloned.1.call-done = bf16[1024,1024]{1,0:T(8,128)(2,1)} async-done(((bf16[256,1024]{1,0:T(8,128)(2,1)}), bf16[1024,1024]{1,0:T(8,128)(2,1)}) %all-gather.7.cloned.1.call-update) | async-done | bytes 2097168 | tf_op jit(solution)/shard_map/all_gather | solution.py:84
  167.9 5.4 fusion.42
  173.3 3.3 fusion.41
  176.6 37.5 %all-gather.9.cloned.1.call-done = bf16[1024,1024]{1,0:T(8,128)(2,1)} async-done(((bf16[256,1024]{1,0:T(8,128)(2,1)}), bf16[1024,1024]{1,0:T(8,128)(2,1)}) %all-gather.9.cloned.1.call-update) | async-done | bytes 2097168 | tf_op jit(solution)/shard_map/all_gather | solution.py:96
  214.1 6.3 %multiply_convert_fusion = (bf16[1024,704]{0,1:T(8,128)(2,1)S(1)}, bf16[1024,704]{0,1:T(8,128)(2,1)}, bf16[1024,704]{0,1:T(8,128)(2,1)S(1)}) fusion(f32[1024,704]{0,1:T(8,128)} %fusion.41, f32[1024,704]{0,1:T(8,128)} %fusion.42, bf16[1024,1024]{1,0:T(8,128)(2,1)} %all-gather.9.cloned.1.call-done, bf16[704,1024]{1,0:T(8,128)(2,1)S(1)} %copy-done), kind=kOutput, calls=%fused_computation.7 | convolution fusion | flops 1480720384 | bytes 13631488 | tf_op jit(solution)/shard_map/td,fd->tf/dot_general | solution.py:98
  220.5 1.8 fusion.43
  222.3 0.5 copy-done.51
  222.9 3.2 add_convert_fusion
  226.1 42.7 %reduce-scatter.9.cloned.1.call-done = bf16[256,1024]{1,0:T(8,128)(2,1)} async-done(((bf16[1024,1024]{1,0:T(8,128)(2,1)}), bf16[256,1024]{1,0:T(8,128)(2,1)}) %reduce-scatter.9.cloned.1.call-update) | async-done | bytes 524304 | tf_op jit(solution)/shard_map/reduce_scatter | solution.py:103
  268.8 2.0 fusion.20
  270.8 0.6 copy-done.44
  271.4 2.5 fusion.37
  274.2 4.9 convolution_convert_fusion.4
  279.1 2.8 convolution_convert_fusion.5
  281.9 2.8 convolution_convert_fusion.6
  284.7 34.7 %all-gather.11.cloned.1.call-done = bf16[1024,1024]{1,0:T(8,128)(2,1)} async-done(((bf16[256,1024]{1,0:T(8,128)(2,1)}), bf16[1024,1024]{1,0:T(8,128)(2,1)}) %all-gather.11.cloned.1.call-update) | async-done | bytes 2097168 | tf_op jit(solution)/shard_map/all_gather | solution.py:114
  319.3 4.1 fusion.38
  323.7 0.3 fusion.34
  324.0 5.1 convolution_convert_fusion.7
  329.1 2.7 select_convert_fusion
  331.8 1.6 fusion.4
  333.4 2.9 fusion.3
  336.3 2.4 convolution_convert_fusion
  338.7 1.4 fusion.39
  340.1 1.1 copy-done.48
  341.2 1.5 convolution_convert_fusion.8
  342.8 5.6 %convolution_convert_fusion.1 = bf16[1024,1024]{1,0:T(8,128)(2,1)} fusion(bf16[1024,1024]{1,0:T(8,128)(2,1)} %copy-done.35, bf16[1024,256]{0,1:T(8,128)(2,1)} %copy-done.52, bf16[1024,256]{0,1:T(8,128)(2,1)S(1)} %bitcast.98, bf16[1024,256]{0,1:T(8,128)(2,1)S(1)} %bitcast.100, bf16[1024,256]{0,1:T(8,128)(2,1)} %bitcast.102), kind=kOutput, calls=%fused_computation.17 | convolution fusion | flops 2156920832 | bytes 6291456 | tf_op jit(solution)/shard_map/tq,cq->tc/dot_general | solution.py:158
  348.6 4.6 convolution_convert_fusion.3
  353.2 101.3 %all-reduce.4.cloned.1.call-done = (bf16[1024,256]{1,0:T(8,128)(2,1)}, bf16[1024,256]{1,0:T(8,128)(2,1)}, bf16[1024,256]{1,0:T(8,128)(2,1)}, bf16[1024,256]{1,0:...) async-done(((bf16[1024,256]{1,0:T(8,128)(2,1)}, bf16[1024,256]{1,0:T(8,128)(2,1)}, ...) | async-done | bytes 6946832 | tf_op jit(solution)/shard_map/psum | solution.py:171
  454.5 2.2 convert_element_type.164
  456.6 2.1 convert_element_type.165
  458.8 1.0 convert_element_type.166
  459.8 1.0 convert_element_type.167
  460.9 1.1 convert_element_type.169
  462.0 1.9 convert_element_type.171
  463.9 1.9 convert_element_type.173
  465.9 1.9 convert_element_type.175
  467.9 33.0 %reduce-scatter.11.cloned.1.call-done = bf16[256,1024]{1,0:T(8,128)(2,1)} async-done(((bf16[1024,1024]{1,0:T(8,128)(2,1)}), bf16[256,1024]{1,0:T(8,128)(2,1)}) %reduce-scatter.11.cloned.1.call-update) | async-done | bytes 524304 | tf_op jit(solution)/shard_map/reduce_scatter | solution.py:157
  500.8 2.0 fusion.24
  502.8 42.2 %all-reduce = (f32[1024]{0:T(1024)}, f32[1024]{0:T(1024)}) all-reduce(f32[1024]{0:T(1024)} %get-tuple-element.14, f32[1024]{0:T(1024)S(1)} %copy-done.42), channel_id=1, replica_groups=mesh['dp'=8,'tensor'=4] {'dp','tensor'}, use_global_device_ids=true, to_apply=%region_19.20 | all-reduce | flops 2048 | bytes 16384 | tf_op jit(solution)/shard_map/psum | solution.py:190
  545.0 0.7 broadcast_multiply_fusion.2
  545.7 1.7 reduce-scatter.7.cloned.1.call-done
  547.4 3.1 fusion.15
  (125 shorter events, 1.6 us)
Async XLA Ops:
  7.2 206.9 %copy-start = (bf16[704,1024]{1,0:T(8,128)(2,1)S(1)}, bf16[704,1024]{1,0:T(8,128)(2,1)}, u32[]{:S(2)}) copy-start(bf16[704,1024]{1,0:T(8,128)(2,1)} %param.22) | copy-start | bytes 4325380
  7.2 4.2 copy-start.30
  7.2 4.2 copy-start.31
  7.2 4.3 copy-start.32
  7.2 52.9 %all-gather.5.cloned.1.call-start = ((), (), s32[]{:S(2)}) async-start(), calls=%async_computation.4 | async-start | bytes 2621440 | tf_op jit(solution)/shard_map/all_gather | solution.py:53
  8.7 0.6 copy-start.43
  11.3 1.0 copy-start.33
  11.3 2.4 copy-start.41
  11.3 107.8 %reduce-scatter.5.cloned.1.call-start = ((), (), s32[]{:S(2)}) async-start(), calls=%async_computation.5 | async-start | bytes 2621440 | tf_op jit(solution)/shard_map/reduce_scatter | solution.py:75
  12.4 1.3 copy-start.35
  14.3 51.7 %copy-start.24 = (pred[1024,1024]{1,0:T(8,128)(4,1)}, pred[1024,1024]{1,0:T(8,128)(4,1)S(1)}, u32[]{:S(2)}) copy-start(pred[1024,1024]{1,0:T(8,128)(4,1)S(1)} %fusion) | copy-start | bytes 3145732
  64.8 7.4 %copy-start.12 = (f32[1024,1024]{0,1:T(8,128)}, f32[1024,1024]{0,1:T(8,128)S(1)}, u32[]{:S(2)}) copy-start(f32[1024,1024]{0,1:T(8,128)S(1)} %fusion.40) | copy-start | bytes 12582916
  64.9 3.9 copy-start.13
  66.0 2.7 copy-start.17
  66.0 2.7 copy-start.19
  68.7 3.3 copy-start.1
  72.0 2.2 copy-start.34
  72.2 1.0 copy-start.11
  73.5 0.8 copy-start.15
  74.3 44.8 %copy-start.2 = (bf16[256,1024]{1,0:T(8,128)(2,1)S(1)}, bf16[256,1024]{1,0:T(8,128)(2,1)}, u32[]{:S(2)}) copy-start(bf16[256,1024]{1,0:T(8,128)(2,1)} %param.13) | copy-start | bytes 1572868
  76.3 44.1 %copy-start.36 = (f32[1024]{0:T(1024)S(1)}, f32[1024]{0:T(1024)}, u32[]{:S(2)}) copy-start(f32[1024]{0:T(1024)} %param.24) | copy-start | bytes 12292
  76.4 91.5 %all-gather.7.cloned.1.call-start = ((), (), s32[]{:S(2)}) async-start(), calls=%async_computation.6 | async-start | bytes 2621440 | tf_op jit(solution)/shard_map/all_gather | solution.py:84
  120.4 52.9 %copy-start.39 = (f32[256]{0:T(256)}, f32[256]{0:T(256)S(1)}, u32[]{:S(2)}) copy-start(f32[256]{0:T(256)S(1)} %add_rsqrt_fusion.1) | copy-start | bytes 3076
  122.5 91.6 %all-gather.9.cloned.1.call-start = ((), (), s32[]{:S(2)}) async-start(), calls=%async_computation.8 | async-start | bytes 2621440 | tf_op jit(solution)/shard_map/all_gather | solution.py:96
  123.0 145.8 %reduce-scatter.9.cloned.1.call-start = ((), (), s32[]{:S(2)}) async-start(), calls=%async_computation.9 | async-start | bytes 2621440 | tf_op jit(solution)/shard_map/reduce_scatter | solution.py:103
  167.9 5.4 copy-start.46
  167.9 5.4 copy-start.49
  214.1 6.4 %copy-start.50 = (bf16[1024,704]{0,1:T(8,128)(2,1)S(1)}, bf16[1024,704]{0,1:T(8,128)(2,1)}, u32[]{:S(2)}) copy-start(bf16[1024,704]{0,1:T(8,128)(2,1)} %param.20) | copy-start | bytes 4325380
  220.4 1.9 copy-start.8
  220.4 1.9 copy-start.10
  220.4 2.4 copy-start.51
  226.0 42.8 %copy-start.3 = (bf16[256,1024]{1,0:T(8,128)(2,1)S(1)}, bf16[256,1024]{1,0:T(8,128)(2,1)}, u32[]{:S(2)}) copy-start(bf16[256,1024]{1,0:T(8,128)(2,1)} %reduce-scatter.5.cloned.1.call-done) | copy-start | bytes 1572868
  226.1 93.3 %all-gather.11.cloned.1.call-start = ((), (), s32[]{:S(2)}) async-start(), calls=%async_computation.10 | async-start | bytes 2621440 | tf_op jit(solution)/shard_map/all_gather | solution.py:114
  270.8 0.6 copy-start.44
  273.9 180.5 %all-reduce.4.cloned.1.call-start = ((), (), s32[]{:S(2)}) async-start(), calls=%async_computation.12 | async-start | bytes 13893632 | tf_op jit(solution)/shard_map/psum | solution.py:171
  274.2 5.0 copy-start.9
  274.2 5.0 copy-start.47
  279.1 2.8 copy-start.4
  279.1 2.8 copy-start.7
  323.4 12.9 %copy-start.52 = (bf16[1024,256]{0,1:T(8,128)(2,1)}, bf16[1024,256]{0,1:T(8,128)(2,1)S(1)}, u32[]{:S(2)}) copy-start(bf16[1024,256]{0,1:T(8,128)(2,1)S(1)} %get-tuple-element.27) | copy-start | bytes 1572868
  323.9 5.1 copy-start.14
  324.0 5.1 copy-start.25
  329.1 2.7 copy-start.20
  331.8 1.6 copy-start.18
  333.4 2.9 copy-start.45
  336.3 2.4 copy-start.29
  338.7 1.4 copy-start.16
  338.7 2.5 copy-start.48
  342.8 158.1 %reduce-scatter.11.cloned.1.call-start = ((), (), s32[]{:S(2)}) async-start(), calls=%async_computation.11 | async-start | bytes 2621440 | tf_op jit(solution)/shard_map/reduce_scatter | solution.py:157
  348.5 198.9 %reduce-scatter.7.cloned.1.call-start = ((), (), s32[]{:S(2)}) async-start(), calls=%async_computation.7 | async-start | bytes 2621440 | tf_op jit(solution)/shard_map/reduce_scatter | solution.py:88
  454.5 4.3 copy-start.28
  454.5 5.4 copy-start.27
  456.6 4.2 copy-start.26
  458.8 3.2 copy-start.23
  462.0 2.0 copy-start.22
  463.9 1.9 copy-start.21
  465.9 35.0 %copy-start.38 = (f32[1024]{0:T(1024)S(1)}, f32[1024]{0:T(1024)}, u32[]{:S(2)}) copy-start(f32[1024]{0:T(1024)} %param.23) | copy-start | bytes 12292
  465.9 36.9 %copy-start.42 = (f32[1024]{0:T(1024)S(1)}, f32[1024]{0:T(1024)}, u32[]{:S(2)}) copy-start(f32[1024]{0:T(1024)} %get-tuple-element.12) | copy-start | bytes 12292
  465.9 81.5 %copy-start.5 = (bf16[256,1024]{1,0:T(8,128)(2,1)S(1)}, bf16[256,1024]{1,0:T(8,128)(2,1)}, u32[]{:S(2)}) copy-start(bf16[256,1024]{1,0:T(8,128)(2,1)} %param.25) | copy-start | bytes 1572868
  465.9 81.5 %copy-start.6 = (bf16[256,1024]{1,0:T(8,128)(2,1)S(1)}, bf16[256,1024]{1,0:T(8,128)(2,1)}, u32[]{:S(2)}) copy-start(bf16[256,1024]{1,0:T(8,128)(2,1)} %reduce-scatter.9.cloned.1.call-done) | copy-start | bytes 1572868
  465.9 81.5 %copy-start.37 = (f32[1024]{0:T(1024)S(1)}, f32[1024]{0:T(1024)}, u32[]{:S(2)}) copy-start(f32[1024]{0:T(1024)} %param.24) | copy-start | bytes 12292
  465.9 81.5 %copy-start.40 = (f32[256]{0:T(256)S(1)}, f32[256]{0:T(256)}, u32[]{:S(2)}) copy-start(f32[256]{0:T(256)} %copy-done.39) | copy-start | bytes 3076
Sparse Core Ops, SparseCore 0:
  11.4 48.6 all-gather.4
  76.5 42.5 reduce-scatter.4
  122.6 45.2 all-gather.6
  169.4 44.6 all-gather.8
  226.2 42.5 reduce-scatter.8
  274.1 45.2 all-gather.10
  342.9 111.5 all-reduce.3
  456.8 43.9 reduce-scatter.10
  503.1 44.1 reduce-scatter.6
where the time goes:
time: 566 us; the launch traced here: 557 us
  waiting for transfers between devices  384 us (68%)
  matrix products  73 us (13%)
  blocking collectives  42.2 us (7%)
  other arithmetic  33 us (6%)
  between operations  14.7 us (3%)
  local copies, waits for them, and re-layouts  9.13 us (2%)
    psum x1, waiting for transfers between devices, per_device(): lax.psum(tuple((part.astype(jnp.bfloat16) for part in (query_grad, key_gr...  101 us
    all_gather x1, waiting for transfers between devices, per_device(): normed_all = lax.all_gather(normed_own, 'tensor', axis=0, tiled=True)  45.8 us
    all_gather x1, waiting for transfers between devices, per_device(): second_all = lax.all_gather(second_own, 'tensor', axis=0, tiled=True)  44.3 us
    reduce_scatter x1, waiting for transfers between devices, per_device(): lax.psum_scatter((jnp.einsum('tf,cf->tc', left_back, left_weight, preferr...  42.7 us
    reduce_scatter x1, waiting for transfers between devices, per_device(): lax.psum_scatter(jnp.dot(gated, out_weight, preferred_element_type=jnp.fl...  42.7 us
    psum x1, blocking collectives, per_device(): lax.psum((first_part, second_part), ('dp', 'tensor'))  42.2 us
    all_gather x1, waiting for transfers between devices, per_device(): down_in = lax.all_gather(cotangent, 'tensor', axis=0, tiled=True)  37.5 us
    all_gather x1, waiting for transfers between devices, per_device(): lax.all_gather(resid_grad.astype(jnp.bfloat16), 'tensor', axis=0, tiled=T...  34.7 us
  transfers between devices with their start and end apart: 9, of which 9 were waited for; matrix products, arithmetic and copies ran while one was open for 8% of the time, Pallas kernels for 0%

commit v1 on v0

--- a/solution.py
+++ b/solution.py
@@ -41,6 +41,21 @@
     norm_second,
     cotangent,
 ):
+
+    def map_spots_for(a0, where_dim):
+        full_n = jax.lax.axis_size("tensor")
+        arr_next = [(to_i - 1, to_i) for to_i in range(1, full_n)] + [(full_n - 1, 0)]
+        back = a0
+        block_list = [back]
+        src_i = 0
+        while src_i < full_n - 1:
+            back = jax.lax.ppermute(back, perm=arr_next, axis_name="tensor")
+            block_list += [back]
+            src_i += 1
+        aux = jnp.concatenate([*reversed(block_list)], where_dim)
+        tile_out = jax.lax.axis_index("tensor")
+        return jnp.roll(aux, (tile_out + 1) * back.shape[where_dim], where_dim)
+
     own_rows = inputs.astype(jnp.float32)
     rows_here, length = segments.shape
     all_tokens = rows_here * length
@@ -81,7 +96,7 @@
     residual = own_rows + branch
     scale_two = rms_scale(residual)
     second_own = (residual * scale_two * norm_second).astype(jnp.bfloat16)
-    second_all = lax.all_gather(second_own, "tensor", axis=0, tiled=True)
+    second_all = map_spots_for(second_own, 0)
     left_out = jnp.dot(second_all, left_weight, preferred_element_type=jnp.float32)
     right_out = jnp.dot(second_all, right_weight, preferred_element_type=jnp.float32)
     product = (left_out * right_out).astype(jnp.bfloat16)

time: 566 us -> 548 us (0.968)
  waiting for transfers between devices: 384 us -> 353 us
  starting transfers between devices: 1.01 us -> 14.8 us
  matrix products: 73 us -> 66 us
  local copies, waits for them, and re-layouts: 9.13 us -> 15.6 us
    ppermute x0 -> x3, waiting for transfers between devices: none -> 51.2 us  [map_spots_for(): back = jax.lax.ppermute(back, perm=arr_next, axis_name='tensor')]
    all_gather x1 -> x0, waiting for transfers between devices: 44.3 us -> none  [per_device(): second_all = lax.all_gather(second_own, 'tensor', axis=0, tiled=True)]
    all_gather x1, waiting for transfers between devices: 37.5 us -> 1.88 us  [per_device(): down_in = lax.all_gather(cotangent, 'tensor', axis=0, tiled=True)]
    ppermute x0 -> x3, starting transfers between devices: none -> 14.3 us  [map_spots_for(): back = jax.lax.ppermute(back, perm=arr_next, axis_name='tensor')]
    unnamed x109 -> x126, local copies, waits for them, and re-layouts: 7.62 us -> 14 us
  transfers between devices with their start and end apart: 9 -> 11, of which waited for: 9 -> 11; matrix products, arithmetic and copies ran while one was open for 8% -> 8% of each run, Pallas kernels for 0% -> 0%
where the time goes in v1:
time: 548 us; the launch traced here: 539 us
  waiting for transfers between devices  353 us (64%)
  matrix products  66 us (12%)
  blocking collectives  42.2 us (8%)
  other arithmetic  32.1 us (6%)
  local copies, waits for them, and re-layouts  15.6 us (3%)
  between operations  15.1 us (3%)
  starting transfers between devices  14.8 us (3%)
    psum x1, waiting for transfers between devices, per_device(): lax.psum(tuple((part.astype(jnp.bfloat16) for part in (query_grad, key_gr...  99.4 us
    ppermute x3, waiting for transfers between devices, map_spots_for(): back = jax.lax.ppermute(back, perm=arr_next, axis_name='tensor')  51.2 us
    all_gather x1, waiting for transfers between devices, per_device(): normed_all = lax.all_gather(normed_own, 'tensor', axis=0, tiled=True)  45.8 us
    reduce_scatter x1, waiting for transfers between devices, per_device(): lax.psum_scatter((jnp.einsum('tf,cf->tc', left_back, left_weight, preferr...  43 us
    psum x1, blocking collectives, per_device(): lax.psum((first_part, second_part), ('dp', 'tensor'))  42.2 us
    reduce_scatter x1, waiting for transfers between devices, per_device(): lax.psum_scatter(jnp.dot(gated, out_weight, preferred_element_type=jnp.fl...  42 us
    all_gather x1, waiting for transfers between devices, per_device(): lax.all_gather(resid_grad.astype(jnp.bfloat16), 'tensor', axis=0, tiled=T...  34.6 us
    reduce_scatter x1, waiting for transfers between devices, per_device(): lax.psum_scatter(jnp.einsum('tq,cq->tc', back_all, joined_weight, preferr...  32.9 us
  transfers between devices with their start and end apart: 11, of which 11 were waited for; matrix products, arithmetic and copies ran while one was open for 8% of the time, Pallas kernels for 0%

profile of v1, /device:TPU:0, one launch (start us, length us, event | category | flops | bytes accessed | tf_op | source)
XLA Modules:
  0.0 538.9 jit_solution(3036371020690239767)
XLA Ops:
  7.3 1.4 fusion.27
  9.3 2.0 fusion.16
  12.4 1.3 copy-done.41
  14.3 45.8 %all-gather.4.cloned.1.call-done = bf16[1024,1024]{1,0:T(8,128)(2,1)} async-done(((bf16[256,1024]{1,0:T(8,128)(2,1)}), bf16[1024,1024]{1,0:T(8,128)(2,1)}) %all-gather.4.cloned.1.call-update) | async-done | bytes 2097168 | tf_op jit(solution)/shard_map/all_gather | solution.py:68
  60.1 4.7 fusion.50
  64.9 1.1 fusion.32
  66.1 2.6 select_convert_fusion.1
  68.8 2.7 multiply_reduce_fusion.2
  73.2 0.8 copy-done.13
  74.0 2.1 convolution_convert_fusion.2
  76.8 42.0 %reduce-scatter.5.cloned.1.call-done = bf16[256,1024]{1,0:T(8,128)(2,1)} async-done(((bf16[1024,1024]{1,0:T(8,128)(2,1)}), bf16[256,1024]{1,0:T(8,128)(2,1)}) %reduce-scatter.5.cloned.1.call-update) | async-done | bytes 524304 | tf_op jit(solution)/shard_map/reduce_scatter | solution.py:90
  118.8 1.3 multiply_reduce_fusion.1
  120.1 1.2 multiply_convert_fusion.3
  121.4 21.3 %collective-permute-done = bf16[256,1024]{1,0:T(8,128)(2,1)S(1)} collective-permute-done((bf16[256,1024]{1,0:T(8,128)(2,1)S(1)}, bf16[256,1024]{1,0:T(8,128)(2,1)S(1)}, u32[]{:S(2)}, u32[]{:S(2)}) %collective-permute-start) | collective-permute-done | bytes 524320 | tf_op jit(solution)/shard_map/ppermute | solution.py:52
  142.7 0.8 copy-done.19
  143.5 3.8 collective-permute-start.1
  147.3 22.6 %collective-permute-done.1 = bf16[256,1024]{1,0:T(8,128)(2,1)} collective-permute-done((bf16[256,1024]{1,0:T(8,128)(2,1)S(1)}, bf16[256,1024]{1,0:T(8,128)(2,1)}, u32[]{:S(2)}, u32[]{:S(2)}) %collective-permute-start.1) | collective-permute-done | bytes 524320 | tf_op jit(solution)/shard_map/ppermute | solution.py:52
  169.9 10.4 %collective-permute-start.2 = (bf16[256,1024]{1,0:T(8,128)(2,1)}, bf16[256,1024]{1,0:T(8,128)(2,1)}, u32[]{:S(2)}, u32[]{:S(2)}) collective-permute-start(bf16[256,1024]{1,0:T(8,128)(2,1)} %collective-permute-done.1), channel_id=1, source_target_pairs={{0,1},{1,2},{2,3},{3,0},{4,5},{5,6},{6,7},{7,4},{8,9},{9,10},{10,1... | collective-permute-start | bytes 1572872 | tf_op jit(solution)/shard_map/ppermute | solution.py:52
  180.4 1.9 all-gather.6.cloned.1.call-done
  182.2 3.7 fusion.51
  185.9 7.3 %collective-permute-done.2 = bf16[256,1024]{1,0:T(8,128)(2,1)} collective-permute-done((bf16[256,1024]{1,0:T(8,128)(2,1)}, bf16[256,1024]{1,0:T(8,128)(2,1)}, u32[]{:S(2)}, u32[]{:S(2)}) %collective-permute-start.2) | collective-permute-done | bytes 524320 | tf_op jit(solution)/shard_map/ppermute | solution.py:52
  193.3 1.1 constant_dynamic-update-slice_fusion.11
  194.3 1.1 constant_dynamic-update-slice_fusion.10
  195.5 1.2 constant_dynamic-update-slice_fusion.7
  196.7 1.1 constant_dynamic-update-slice_fusion.6
  197.9 1.7 fusion.5
  199.8 3.0 multiply_convert_fusion
  202.9 1.9 fusion.52
  204.8 3.3 add_convert_fusion
  208.1 43.0 %reduce-scatter.9.cloned.1.call-done = bf16[256,1024]{1,0:T(8,128)(2,1)} async-done(((bf16[1024,1024]{1,0:T(8,128)(2,1)}), bf16[256,1024]{1,0:T(8,128)(2,1)}) %reduce-scatter.9.cloned.1.call-update) | async-done | bytes 524304 | tf_op jit(solution)/shard_map/reduce_scatter | solution.py:118
  251.2 2.0 fusion.26
  253.2 2.3 fusion.47
  255.8 5.0 convolution_convert_fusion.4
  260.8 2.8 convolution_convert_fusion.5
  263.6 2.8 convolution_convert_fusion.6
  266.4 34.6 %all-gather.8.cloned.1.call-done = bf16[1024,1024]{1,0:T(8,128)(2,1)} async-done(((bf16[256,1024]{1,0:T(8,128)(2,1)}), bf16[1024,1024]{1,0:T(8,128)(2,1)}) %all-gather.8.cloned.1.call-update) | async-done | bytes 2097168 | tf_op jit(solution)/shard_map/all_gather | solution.py:129
  301.0 3.8 fusion.48
  305.3 5.1 convolution_convert_fusion.7
  310.4 2.6 select_convert_fusion
  313.1 1.6 fusion.10
  314.7 2.9 fusion.9
  317.6 2.4 convolution_convert_fusion
  320.0 1.4 fusion.49
  321.4 1.1 copy-done.54
  322.6 1.5 convolution_convert_fusion.8
  324.1 1.0 copy-done.57
  325.1 5.3 convolution_convert_fusion.1
  330.5 1.3 copy-done.27
  331.8 4.6 convolution_convert_fusion.3
  336.4 99.4 %all-reduce.4.cloned.1.call-done = (bf16[1024,256]{1,0:T(8,128)(2,1)}, bf16[1024,256]{1,0:T(8,128)(2,1)}, bf16[1024,256]{1,0:T(8,128)(2,1)}, bf16[1024,256]{1,0:...) async-done(((bf16[1024,256]{1,0:T(8,128)(2,1)}, bf16[1024,256]{1,0:T(8,128)(2,1)}, ...) | async-done | bytes 6946832 | tf_op jit(solution)/shard_map/psum | solution.py:186
  435.8 2.2 convert_element_type.164
  438.0 2.1 convert_element_type.165
  440.1 1.0 convert_element_type.166
  441.2 1.0 convert_element_type.167
  442.2 1.1 convert_element_type.169
  443.3 1.9 convert_element_type.171
  445.3 1.9 convert_element_type.173
  447.3 1.9 convert_element_type.175
  449.3 32.9 %reduce-scatter.11.cloned.1.call-done = bf16[256,1024]{1,0:T(8,128)(2,1)} async-done(((bf16[1024,1024]{1,0:T(8,128)(2,1)}), bf16[256,1024]{1,0:T(8,128)(2,1)}) %reduce-scatter.11.cloned.1.call-update) | async-done | bytes 524304 | tf_op jit(solution)/shard_map/reduce_scatter | solution.py:172
  482.2 2.0 fusion.30
  484.2 42.2 %all-reduce = (f32[1024]{0:T(1024)}, f32[1024]{0:T(1024)}) all-reduce(f32[1024]{0:T(1024)S(1)} %get-tuple-element.14, f32[1024]{0:T(1024)S(1)} %copy-done.49), channel_id=1, replica_groups=mesh['dp'=8,'tensor'=4] {'dp','tensor'}, use_global_device_ids=true, to_apply=%region_19.20 | all-reduce | flops 2048 | bytes 16384 | tf_op jit(solution)/shard_map/psum | solution.py:205
  526.4 0.8 broadcast_multiply_fusion.2
  527.1 1.5 reduce-scatter.7.cloned.1.call-done
  528.7 3.1 fusion.21
  (146 shorter events, 6.4 us)
Async XLA Ops:
  7.2 192.7 %copy-start = (bf16[1024,704]{0,1:T(8,128)(2,1)S(1)}, bf16[1024,704]{0,1:T(8,128)(2,1)}, u32[]{:S(2)}) copy-start(bf16[1024,704]{0,1:T(8,128)(2,1)} %param.20) | copy-start | bytes 4325380
  7.2 4.2 copy-start.36
  7.2 4.2 copy-start.37
  7.2 4.3 copy-start.38
  7.2 52.9 %all-gather.4.cloned.1.call-start = ((), (), s32[]{:S(2)}) async-start(), calls=%async_computation.4 | async-start | bytes 2621440 | tf_op jit(solution)/shard_map/all_gather | solution.py:68
  11.3 1.0 copy-start.39
  11.3 2.4 copy-start.48
  11.3 107.5 %reduce-scatter.5.cloned.1.call-start = ((), (), s32[]{:S(2)}) async-start(), calls=%async_computation.5 | async-start | bytes 2621440 | tf_op jit(solution)/shard_map/reduce_scatter | solution.py:90
  12.4 1.3 copy-start.41
  14.3 51.7 %copy-start.31 = (pred[1024,1024]{1,0:T(8,128)(4,1)}, pred[1024,1024]{1,0:T(8,128)(4,1)S(1)}, u32[]{:S(2)}) copy-start(pred[1024,1024]{1,0:T(8,128)(4,1)S(1)} %fusion) | copy-start | bytes 3145732
  64.8 7.4 %copy-start.10 = (f32[1024,1024]{0,1:T(8,128)}, f32[1024,1024]{0,1:T(8,128)S(1)}, u32[]{:S(2)}) copy-start(f32[1024,1024]{0,1:T(8,128)S(1)} %fusion.50) | copy-start | bytes 12582916
  64.9 3.9 copy-start.11
  66.0 2.7 copy-start.15
  66.0 2.7 copy-start.17
  68.7 3.3 copy-start.2
  72.1 1.9 copy-start.40
  76.0 42.8 %copy-start.3 = (bf16[256,1024]{1,0:T(8,128)(2,1)S(1)}, bf16[256,1024]{1,0:T(8,128)(2,1)}, u32[]{:S(2)}) copy-start(bf16[256,1024]{1,0:T(8,128)(2,1)} %param.13) | copy-start | bytes 1572868
  76.1 106.2 %all-gather.6.cloned.1.call-start = ((), (), s32[]{:S(2)}) async-start(), calls=%async_computation.7 | async-start | bytes 2621440 | tf_op jit(solution)/shard_map/all_gather | solution.py:111
  76.8 174.4 %reduce-scatter.9.cloned.1.call-start = ((), (), s32[]{:S(2)}) async-start(), calls=%async_computation.8 | async-start | bytes 2621440 | tf_op jit(solution)/shard_map/reduce_scatter | solution.py:118
  120.1 49.8 %copy-start.45 = (f32[256]{0:T(256)}, f32[256]{0:T(256)S(1)}, u32[]{:S(2)}) copy-start(f32[256]{0:T(256)S(1)} %add_rsqrt_fusion.1) | copy-start | bytes 3076
  121.4 21.3 %collective-permute-start = (bf16[256,1024]{1,0:T(8,128)(2,1)S(1)}, bf16[256,1024]{1,0:T(8,128)(2,1)S(1)}, u32[]{:S(2)}, u32[]{:S(2)}) collective-permute-start(bf16[256,1024]{1,0:T(8,128)(2,1)S(1)} %multiply_convert_fusion.3), channel_id=1, source_target_pairs={{0,1},{1,2},{2,3},{3,0},{4,5},{5,6},{6,7},{7,4},{8,9},{9,10},{10,1... | collective-permute-start | bytes 1572872 | tf_op jit(solution)/shard_map/ppermute | solution.py:52
  143.5 26.4 %collective-permute-start.1 = (bf16[256,1024]{1,0:T(8,128)(2,1)S(1)}, bf16[256,1024]{1,0:T(8,128)(2,1)}, u32[]{:S(2)}, u32[]{:S(2)}) collective-permute-start(bf16[256,1024]{1,0:T(8,128)(2,1)S(1)} %collective-permute-done), channel_id=1, source_target_pairs={{0,1},{1,2},{2,3},{3,0},{4,5},{5,6},{6,7},{7,4},{8,9},{9,10},{10,1... | collective-permute-start | bytes 1572872 | tf_op jit(solution)/shard_map/ppermute | solution.py:52
  169.9 23.3 %collective-permute-start.2 = (bf16[256,1024]{1,0:T(8,128)(2,1)}, bf16[256,1024]{1,0:T(8,128)(2,1)}, u32[]{:S(2)}, u32[]{:S(2)}) collective-permute-start(bf16[256,1024]{1,0:T(8,128)(2,1)} %collective-permute-done.1), channel_id=1, source_target_pairs={{0,1},{1,2},{2,3},{3,0},{4,5},{5,6},{6,7},{7,4},{8,9},{9,10},{10,1... | collective-permute-start | bytes 1572872 | tf_op jit(solution)/shard_map/ppermute | solution.py:52
  185.9 9.5 %copy-start.20 = (bf16[256,1024]{1,0:T(8,128)(2,1)S(1)}, bf16[256,1024]{1,0:T(8,128)(2,1)}, u32[]{:S(2)}) copy-start(bf16[256,1024]{1,0:T(8,128)(2,1)} %copy-done.19) | copy-start | bytes 1572868
  195.5 2.4 copy-start.55
  197.9 1.9 copy-start.21
  202.9 1.9 copy-start.28
  202.9 1.9 copy-start.30
  208.1 43.1 %copy-start.4 = (bf16[256,1024]{1,0:T(8,128)(2,1)S(1)}, bf16[256,1024]{1,0:T(8,128)(2,1)}, u32[]{:S(2)}) copy-start(bf16[256,1024]{1,0:T(8,128)(2,1)} %reduce-scatter.5.cloned.1.call-done) | copy-start | bytes 1572868
  208.1 43.1 %copy-start.42 = (f32[1024]{0:T(1024)S(1)}, f32[1024]{0:T(1024)}, u32[]{:S(2)}) copy-start(f32[1024]{0:T(1024)} %param.24) | copy-start | bytes 12292
  208.1 43.1 %copy-start.46 = (f32[256]{0:T(256)S(1)}, f32[256]{0:T(256)}, u32[]{:S(2)}) copy-start(f32[256]{0:T(256)} %copy-done.45) | copy-start | bytes 3076
  208.1 45.1 %copy-start.5 = (bf16[256,1024]{1,0:T(8,128)(2,1)S(1)}, bf16[256,1024]{1,0:T(8,128)(2,1)}, u32[]{:S(2)}) copy-start(bf16[256,1024]{1,0:T(8,128)(2,1)} %param.25) | copy-start | bytes 1572868
  208.1 92.9 %all-gather.8.cloned.1.call-start = ((), (), s32[]{:S(2)}) async-start(), calls=%async_computation.9 | async-start | bytes 2621440 | tf_op jit(solution)/shard_map/all_gather | solution.py:129
  253.2 2.3 copy-start.51
  255.5 5.2 copy-start.29
  255.6 180.3 %all-reduce.4.cloned.1.call-start = ((), (), s32[]{:S(2)}) async-start(), calls=%async_computation.11 | async-start | bytes 13893632 | tf_op jit(solution)/shard_map/psum | solution.py:186
  255.8 5.0 copy-start.22
  260.8 2.8 copy-start.26
  260.8 2.8 copy-start.53
  263.6 37.4 %copy-start.9 = (f32[1,1024,4,64]{1,3,2,0:T(8,128)S(1)}, f32[1,1024,4,64]{1,3,2,0:T(8,128)}, u32[]{:S(2)}) copy-start(f32[1,1024,4,64]{1,3,2,0:T(8,128)} %copy-done.8) | copy-start | bytes 3145732
  304.7 12.9 %copy-start.56 = (bf16[1024,256]{0,1:T(8,128)(2,1)}, bf16[1024,256]{0,1:T(8,128)(2,1)S(1)}, u32[]{:S(2)}) copy-start(bf16[1024,256]{0,1:T(8,128)(2,1)S(1)} %get-tuple-element.27) | copy-start | bytes 1572868
  305.3 5.1 copy-start.12
  305.3 5.1 copy-start.32
  310.4 2.7 copy-start.18
  313.1 1.6 copy-start.16
  314.7 2.9 copy-start.52
  320.0 1.4 copy-start.14
  320.0 2.5 copy-start.54
  324.1 158.1 %reduce-scatter.11.cloned.1.call-start = ((), (), s32[]{:S(2)}) async-start(), calls=%async_computation.10 | async-start | bytes 2621440 | tf_op jit(solution)/shard_map/reduce_scatter | solution.py:172
  330.4 1.4 copy-start.27
  330.5 198.2 %reduce-scatter.7.cloned.1.call-start = ((), (), s32[]{:S(2)}) async-start(), calls=%async_computation.6 | async-start | bytes 2621440 | tf_op jit(solution)/shard_map/reduce_scatter | solution.py:103
  435.8 4.3 copy-start.35
  435.8 5.4 copy-start.34
  438.0 4.2 copy-start.33
  440.1 3.2 copy-start.25
  443.3 2.0 copy-start.24
  445.3 1.9 copy-start.23
  447.3 34.9 %copy-start.44 = (f32[1024]{0:T(1024)S(1)}, f32[1024]{0:T(1024)}, u32[]{:S(2)}) copy-start(f32[1024]{0:T(1024)} %param.23) | copy-start | bytes 12292
  447.3 36.9 %copy-start.49 = (f32[1024]{0:T(1024)S(1)}, f32[1024]{0:T(1024)}, u32[]{:S(2)}) copy-start(f32[1024]{0:T(1024)} %get-tuple-element.12) | copy-start | bytes 12292
  447.3 81.4 %copy-start.6 = (bf16[256,1024]{1,0:T(8,128)(2,1)S(1)}, bf16[256,1024]{1,0:T(8,128)(2,1)}, u32[]{:S(2)}) copy-start(bf16[256,1024]{1,0:T(8,128)(2,1)} %param.25) | copy-start | bytes 1572868
  447.3 81.4 %copy-start.7 = (bf16[256,1024]{1,0:T(8,128)(2,1)S(1)}, bf16[256,1024]{1,0:T(8,128)(2,1)}, u32[]{:S(2)}) copy-start(bf16[256,1024]{1,0:T(8,128)(2,1)} %reduce-scatter.9.cloned.1.call-done) | copy-start | bytes 1572868
  447.3 81.4 %copy-start.43 = (f32[1024]{0:T(1024)S(1)}, f32[1024]{0:T(1024)}, u32[]{:S(2)}) copy-start(f32[1024]{0:T(1024)} %param.24) | copy-start | bytes 12292
  447.3 81.4 %copy-start.47 = (f32[256]{0:T(256)S(1)}, f32[256]{0:T(256)}, u32[]{:S(2)}) copy-start(f32[256]{0:T(256)} %copy-done.45) | copy-start | bytes 3076
  526.3 5.5 %copy-start.1 = (bf16[1024,704]{0,1:T(8,128)(2,1)S(1)}, bf16[1024,704]{0,1:T(8,128)(2,1)}, u32[]{:S(2)}) copy-start(bf16[1024,704]{0,1:T(8,128)(2,1)} %param.20) | copy-start | bytes 4325380
  (5 other events, 4.2 us)
Sparse Core Ops, SparseCore 0:
  11.4 48.6 all-gather.3
  76.2 42.5 reduce-scatter.4
  120.5 61.7 all-gather.5
  208.2 42.9 reduce-scatter.8
  255.7 45.2 all-gather.7
  324.2 111.5 all-reduce.3
  438.2 43.9 reduce-scatter.10
  484.5 44.1 reduce-scatter.6
